TPU v7x, 128 devices: a whole 4x4x4 slice. The times are simulated.
128 devices in a mesh: row: 8 (over z, core), col: 8 (over y_hi, x), freq: 2 (over y_lo).
Axes of the slice: x: 4, y: 4 (y_hi: 2, y_lo: 2; y = y_hi * 2 + y_lo), z: 4, core: 2. Of those that a mesh axis runs over, the one named last changes fastest.
Arguments:
- pair_elements: bfloat16 [2, 1024, 8192], P(None, ('row', 'freq'), 'col'), may hold values from -1.59375 to 1.59375
- transitions: int32 [3, 1024], replicated, may hold values from 0 to 63, as said below
- energies: float32 [16, 64], replicated, may hold values from -3 to 3
- occupations: int32 [16, 64], replicated, may hold values from 0 to 2
- frequencies: float32 [4], P('freq'), may hold values from 0.2 to 2
Outputs:
- chi_zero: float32 [4, 2, 8192, 8192], P('freq', None, 'row', 'col')
Inputs may be any that keep to these rules, and one draw needn't show every extreme that they name: transitions[0] is a k-point below 16, transitions[1] a valence band below 32, transitions[2] a conduction band of 32 to 63.
All inputs are finite; a program needn't handle non-finite values.
Results may differ from a plain program's by a relative error of at most 0.0028.
Values may be sent and summed in bfloat16 or wider, within the bound.
A program may use at most 128 MiB of HBM per device.

v0:
```python
import jax
import jax.numpy as jnp
from jax import lax
from jax.sharding import PartitionSpec as P


def broadcast(value, axis, source):
    kept = jnp.where(lax.axis_index(axis) == source, value, 0).astype(value.dtype)
    return lax.psum(kept, axis)


def lookup(table, flat_rows):
    flat = table.reshape(-1)
    onehot = (flat_rows[:, None] == jnp.arange(flat.shape[0], dtype=jnp.int32)[None, :]).astype(
        jnp.float32
    )
    return jnp.dot(onehot, flat, precision=lax.Precision.HIGHEST)


def weights(transitions, energies, occupations, frequencies):
    bands = energies.shape[1]
    kpoint = transitions[0]
    valence_rows = kpoint * bands + transitions[1]
    conduction_rows = kpoint * bands + transitions[2]
    gap = lookup(energies, conduction_rows) - lookup(energies, valence_rows)
    occ_float = occupations.astype(jnp.float32)
    filled = lookup(occ_float, valence_rows) - lookup(occ_float, conduction_rows)
    return (
        filled[None, :]
        * 2.0
        * gap[None, :]
        / (gap[None, :] * gap[None, :] + frequencies[:, None] * frequencies[:, None])
    )


def contribute(left, right, weight_block):
    right_both = jnp.concatenate([right[0], right[1]], 0)
    dims = (((0,), (0,)), ((), ()))
    results = []
    for index in range(weight_block.shape[0]):
        scaled = (left.astype(jnp.float32) * weight_block[index][None, :, None]).astype(
            jnp.bfloat16
        )
        real_left = jnp.concatenate([scaled[0], scaled[1]], 0)
        imag_left = jnp.concatenate([scaled[1], -scaled[0]], 0)
        real_component = lax.dot_general(
            real_left, right_both, dims, preferred_element_type=jnp.float32
        )
        imag_part = lax.dot_general(imag_left, right_both, dims, preferred_element_type=jnp.float32)
        results.append(jnp.stack([real_component, imag_part], 0))
    return jnp.stack(results, 0)


def body(pair_elements, transitions, energies, occupations, frequencies):
    weight = weights(transitions, energies, occupations, frequencies)
    column_panel = lax.all_gather(pair_elements, ("row", "freq"), axis=1, tiled=True)
    row_panel = broadcast(column_panel, "col", lax.axis_index("row"))
    chi_zero = contribute(row_panel, column_panel, weight)
    return chi_zero


def solution(mesh):
    in_specs = (P(None, ("row", "freq"), "col"), P(), P(), P(), P("freq"))
    out_specs = P("freq", None, "row", "col")
    return jax.shard_map(body, mesh=mesh, in_specs=in_specs, out_specs=out_specs, check_vma=False)
```

profile of v0, /device:TPU:1, one launch (start us, length us, event | category | flops | bytes accessed | tf_op | source)
XLA Modules:
  0.0 221.2 jit_solution(16224956101808167653)
XLA Ops:
  6.5 0.7 all-gather.2.cloned.1.call-update
  7.3 54.5 %all-gather.2.cloned.1.call-done = bf16[2,1024,1024]{2,1,0:T(8,128)(2,1)} async-done(((bf16[2,64,1024]{2,1,0:T(8,128)(2,1)}), bf16[2,1024,1024]{2,1,0:T(8,128)(2,1)}) %all-gather.2.cloned.1.call-update) | async-done | bytes 4194320 | tf_op jit(solution)/shard_map/all_gather | solution.py:56
  61.8 2.3 %broadcast_select_fusion = bf16[2,1024,1024]{2,1,0:T(8,128)(2,1)} fusion(bf16[2,1024,1024]{2,1,0:T(8,128)(2,1)} %all-gather.2.cloned.1.call-done, pred[]{:T(512)S(6)} %eq.14), kind=kLoop, calls=%fused_computation.30 | loop fusion | flops 2097152 | bytes 8388609 | tf_op jit(solution)/shard_map/jit(_where)/select_n | solution.py:8
  64.1 0.6 copy-done.5
  64.8 0.1 reshape.45
  64.9 0.1 reshape.41
  65.0 2.0 fusion.18
  67.0 2.0 fusion.19
  69.0 2.0 fusion.21
  71.0 2.0 fusion.20
  73.0 0.1 add_divide_fusion
  73.2 1.8 slice_bitcast_fusion.3
  75.0 102.2 %all-reduce.2.cloned.1.call-done = bf16[2,1024,1024]{2,1,0:T(8,128)(2,1)} async-done(((bf16[2,1024,1024]{2,1,0:T(8,128)(2,1)}), bf16[2,1024,1024]{2,1,0:T(8,128)(2,1)}) %all-reduce.2.cloned.1.call-update) | async-done | bytes 4194320 | tf_op jit(solution)/shard_map/psum | solution.py:9
  177.2 2.9 %fusion = (bf16[2,1024,1024]{2,1,0:T(8,128)(2,1)S(1)}, bf16[2,1024,1024]{2,1,0:T(8,128)(2,1)S(1)}) fusion(bf16[2,1024,1024]{2,1,0:T(8,128)(2,1)} %all-reduce.2.cloned.1.call-done, f32[1024]{0:T(1024)S(1)} %bitcast.40, f32[1024]{0:T(1024)S(1)} %bitcast.41), kind=kLoop, calls=%fused_computation.3 | loop fusion | flops 10485760 | bytes 12591104 | tf_op jit(solution)/shard_map/convert_element_type | solution.py:41
  180.1 0.3 fusion.42
  180.4 1.1 slice_bitcast_fusion.1
  181.6 0.4 copy-done.1
  182.0 4.7 %fusion.25 = f32[1,1024,1024]{2,1,0:T(8,128)S(1)} fusion(bf16[1024,1024]{1,0:T(8,128)(2,1)S(1)} %get-tuple-element.10, bf16[1024,1024]{1,0:T(8,128)(2,1)S(1)} %get-tuple-element.9, bf16[1024,1024]{1,0:T(8,128)(2,1)S(1)} %copy-done.1, bf16[1024,1024]{1,0:T(8,128)(2,1)S(1)} %get-tuple-element.11), kind=kOutput, calls=%fused_computation.32 | convolution fusion | flops 4311744512 | bytes 12582912 | tf_op jit(solution)/shard_map/dot_general | solution.py:46
  186.7 4.7 %fusion.22 = f32[1,1024,1024]{2,1,0:T(8,128)S(1)} fusion(bf16[1024,1024]{1,0:T(8,128)(2,1)S(1)} %get-tuple-element.22, bf16[1024,1024]{1,0:T(8,128)(2,1)S(1)} %get-tuple-element.10, bf16[1024,1024]{1,0:T(8,128)(2,1)S(1)} %copy-done.1, bf16[1024,1024]{1,0:T(8,128)(2,1)S(1)} %get-tuple-element.11), kind=kOutput, calls=%fused_computation.31 | convolution fusion | flops 4311744512 | bytes 12582912 | tf_op jit(solution)/shard_map/dot_general | solution.py:49
  191.3 4.9 %fusion.31 = f32[1,1024,1024]{2,1,0:T(8,128)S(1)} fusion(bf16[1024,1024]{1,0:T(8,128)(2,1)S(1)} %get-tuple-element.19, bf16[1024,1024]{1,0:T(8,128)(2,1)S(1)} %get-tuple-element.20, bf16[1024,1024]{1,0:T(8,128)(2,1)S(1)} %copy-done.1, bf16[1024,1024]{1,0:T(8,128)(2,1)S(1)} %get-tuple-element.11), kind=kOutput, calls=%fused_computation.34 | convolution fusion | flops 4311744512 | bytes 12582912 | tf_op jit(solution)/shard_map/dot_general | solution.py:46
  196.3 6.8 %fusion.28 = f32[1,1024,1024]{2,1,0:T(8,128)} fusion(bf16[1024,1024]{1,0:T(8,128)(2,1)S(1)} %get-tuple-element.21, bf16[1024,1024]{1,0:T(8,128)(2,1)S(1)} %get-tuple-element.19, bf16[1024,1024]{1,0:T(8,128)(2,1)S(1)} %copy-done.1, bf16[1024,1024]{1,0:T(8,128)(2,1)S(1)} %get-tuple-element.11), kind=kOutput, calls=%fused_computation.33 | convolution fusion | flops 4311744512 | bytes 12582912 | tf_op jit(solution)/shard_map/dot_general | solution.py:49
  203.0 1.7 maximum_bitcast_fusion.1
  204.7 3.4 %maximum_bitcast_fusion = f32[1,2,1024,1024]{3,2,1,0:T(8,128)S(1)} fusion(f32[1,1024,1024]{2,1,0:T(8,128)} %fusion.28, f32[1,1024,1024]{2,1,0:T(8,128)S(1)} %fusion.31), kind=kLoop, calls=%fused_computation.5 | loop fusion | flops 2097152 | bytes 16777216 | tf_op jit(solution)/shard_map/stack | solution.py:51
  208.1 6.2 %pad_maximum_fusion = f32[2,2,1024,1024]{3,2,1,0:T(8,128)} fusion(f32[1,2,1024,1024]{3,2,1,0:T(8,128)S(1)} %maximum_bitcast_fusion.1, f32[1,2,1024,1024]{3,2,1,0:T(8,128)S(1)} %maximum_bitcast_fusion), kind=kLoop, calls=%fused_computation | loop fusion | flops 4194304 | bytes 33554432 | tf_op jit(solution)/shard_map/stack | solution.py:51
  (18 shorter events, 0.2 us)
Async XLA Ops:
  6.5 55.3 %all-gather.2.cloned.1.call-start = ((), (), s32[]{:S(2)}) async-start(), calls=%async_computation | async-start | bytes 4456448 | tf_op jit(solution)/shard_map/all_gather | solution.py:56
  7.3 169.9 %all-reduce.2.cloned.1.call-start = ((), (), s32[]{:S(2)}) async-start(), calls=%async_computation.1 | async-start | bytes 8388608 | tf_op jit(solution)/shard_map/psum | solution.py:9
  64.1 0.7 copy-start.5
  64.1 0.7 copy-start.3
  64.1 0.8 copy-start.4
  64.1 0.9 copy-start.2
  65.0 8.2 %copy-start = (bf16[2,1024,1024]{2,1,0:T(8,128)(2,1)S(1)}, bf16[2,1024,1024]{2,1,0:T(8,128)(2,1)}, u32[]{:S(2)}) copy-start(bf16[2,1024,1024]{2,1,0:T(8,128)(2,1)} %all-gather.2.cloned.1.call-done) | copy-start | bytes 12582916
  180.4 1.6 copy-start.1
Sparse Core Ops, SparseCore 0:
  9.0 52.7 all-gather.1
  64.3 112.8 all-reduce.1
where the time goes:
time: 221 us
  waiting for transfers between devices  157 us (71%)
  matrix products  29 us (13%)
  other arithmetic  17 us (8%)
  between operations  13.5 us (6%)
  local copies, waits for them, and re-layouts  4.23 us (2%)
    psum x1, waiting for transfers between devices, broadcast(): return lax.psum(kept, axis)  102 us
    all_gather x1, waiting for transfers between devices, body(): lax.all_gather(pair_elements, ('row', 'freq'), axis=1, tiled=True)  54.5 us
    dot_general x2, matrix products, contribute(): lax.dot_general(imag_left, right_both, dims, preferred_element_type=jnp.f...  11.4 us
    another operation x3, other arithmetic, contribute(): return jnp.stack(results, 0)  11.3 us
    dot_general x2, matrix products, contribute(): lax.dot_general(real_left, right_both, dims, preferred_element_type=jnp.f...  9.55 us
    dot_general x4, matrix products, lookup(): return jnp.dot(onehot, flat, precision=lax.Precision.HIGHEST)  8.03 us
  transfers between devices with their start and end apart: 2, of which 2 were waited for; matrix products, arithmetic and copies ran while one was open for 5% of the time, Pallas kernels for 0%

commit v1 on v0

--- a/solution.py
+++ b/solution.py
@@ -4,9 +4,15 @@
 from jax.sharding import PartitionSpec as P
 
 
+def add_all(x, axis):
+    parts = lax.all_gather(x, axis, axis=0, tiled=False)
+    result = parts.sum(axis=0)
+    return result
+
+
 def broadcast(value, axis, source):
     kept = jnp.where(lax.axis_index(axis) == source, value, 0).astype(value.dtype)
-    return lax.psum(kept, axis)
+    return add_all(kept, axis)
 
 
 def lookup(table, flat_rows):

time: 221 us -> 465 us (2.10)
  waiting for transfers between devices: 157 us -> 387 us
  other arithmetic: 17 us -> 31.2 us
    all_gather x0 -> x1, waiting for transfers between devices: none -> 331 us  [add_all(): parts = lax.all_gather(x, axis, axis=0, tiled=False)]
    psum x1 -> x0, waiting for transfers between devices: 102 us -> none  [broadcast(): return lax.psum(kept, axis)]
    reduce_sum x0 -> x1, other arithmetic: none -> 14.2 us  [add_all(): result = parts.sum(axis=0)]
  transfers between devices with their start and end apart: 2 -> 2, of which waited for: 2 -> 2; matrix products, arithmetic and copies ran while one was open for 5% -> 2% of each run, Pallas kernels for 0% -> 0%
where the time goes in v1:
time: 465 us
  waiting for transfers between devices  387 us (83%)
  other arithmetic  31.2 us (7%)
  matrix products  29 us (6%)
  between operations  13.5 us (3%)
    all_gather x1, waiting for transfers between devices, add_all(): parts = lax.all_gather(x, axis, axis=0, tiled=False)  331 us
    all_gather x1, waiting for transfers between devices, body(): lax.all_gather(pair_elements, ('row', 'freq'), axis=1, tiled=True)  54.5 us
    reduce_sum x1, other arithmetic, add_all(): result = parts.sum(axis=0)  14.2 us
    dot_general x2, matrix products, contribute(): lax.dot_general(real_left, right_both, dims, preferred_element_type=jnp.f...  11.4 us
    another operation x3, other arithmetic, contribute(): return jnp.stack(results, 0)  11.3 us
    dot_general x2, matrix products, contribute(): lax.dot_general(imag_left, right_both, dims, preferred_element_type=jnp.f...  9.56 us
  transfers between devices with their start and end apart: 2, of which 2 were waited for; matrix products, arithmetic and copies ran while one was open for 2% of the time, Pallas kernels for 0%

profile of v1, /device:TPU:1, one launch (start us, length us, event | category | flops | bytes accessed | tf_op | source)
XLA Modules:
  0.0 464.5 jit_solution(5997450776059891514)
XLA Ops:
  6.5 0.7 all-gather.4.cloned.1.call-update
  7.3 54.5 %all-gather.4.cloned.1.call-done = bf16[2,1024,1024]{2,1,0:T(8,128)(2,1)} async-done(((bf16[2,64,1024]{2,1,0:T(8,128)(2,1)}), bf16[2,1024,1024]{2,1,0:T(8,128)(2,1)}) %all-gather.4.cloned.1.call-update) | async-done | bytes 4194320 | tf_op jit(solution)/shard_map/all_gather | solution.py:62
  61.8 2.3 broadcast_select_fusion
  64.1 0.7 copy-done.4
  64.8 0.1 reshape.42
  65.0 2.0 fusion.21
  67.0 2.0 fusion.19
  69.0 2.0 fusion.18
  71.0 2.0 fusion.20
  73.0 0.1 add_divide_fusion
  73.2 1.8 slice_bitcast_fusion.3
  74.9 331.4 %all-gather.6.cloned.1.call-done = bf16[16,1024,1024]{2,1,0:T(8,128)(2,1)} async-done(((bf16[2,1024,1024]{2,1,0:T(8,128)(2,1)}), bf16[16,1024,1024]{2,1,0:T(8,128)(2,1)}) %all-gather.6.cloned.1.call-update) | async-done | bytes 33554448 | tf_op jit(solution)/shard_map/all_gather | solution.py:8
  406.3 14.2 %reduce_sum.12 = bf16[2,1024,1024]{2,1,0:T(8,128)(2,1)} reduce(bf16[8,2,1024,1024]{3,2,1,0:T(8,128)(2,1)} %bitcast.41, bf16[]{:T(256)} %constant.16.clone.1), dimensions={0}, to_apply=%region_0.1 | reduce | flops 14680064 | bytes 37748736 | tf_op jit(solution)/shard_map/reduce_sum | solution.py:9
  420.5 2.9 fusion
  423.5 0.3 fusion.42
  423.7 1.1 slice_bitcast_fusion.1
  424.9 0.4 copy-done.1
  425.3 4.7 %fusion.22 = f32[1,1024,1024]{2,1,0:T(8,128)S(1)} fusion(bf16[1024,1024]{1,0:T(8,128)(2,1)S(1)} %get-tuple-element.22, bf16[1024,1024]{1,0:T(8,128)(2,1)S(1)} %get-tuple-element.10, bf16[1024,1024]{1,0:T(8,128)(2,1)S(1)} %copy-done.1, bf16[1024,1024]{1,0:T(8,128)(2,1)S(1)} %get-tuple-element.11), kind=kOutput, calls=%fused_computation.31 | convolution fusion | flops 4311744512 | bytes 12582912 | tf_op jit(solution)/shard_map/dot_general | solution.py:55
  430.0 4.7 %fusion.25 = f32[1,1024,1024]{2,1,0:T(8,128)S(1)} fusion(bf16[1024,1024]{1,0:T(8,128)(2,1)S(1)} %get-tuple-element.10, bf16[1024,1024]{1,0:T(8,128)(2,1)S(1)} %get-tuple-element.9, bf16[1024,1024]{1,0:T(8,128)(2,1)S(1)} %copy-done.1, bf16[1024,1024]{1,0:T(8,128)(2,1)S(1)} %get-tuple-element.11), kind=kOutput, calls=%fused_computation.32 | convolution fusion | flops 4311744512 | bytes 12582912 | tf_op jit(solution)/shard_map/dot_general | solution.py:52
  434.7 4.9 %fusion.28 = f32[1,1024,1024]{2,1,0:T(8,128)S(1)} fusion(bf16[1024,1024]{1,0:T(8,128)(2,1)S(1)} %get-tuple-element.21, bf16[1024,1024]{1,0:T(8,128)(2,1)S(1)} %get-tuple-element.19, bf16[1024,1024]{1,0:T(8,128)(2,1)S(1)} %copy-done.1, bf16[1024,1024]{1,0:T(8,128)(2,1)S(1)} %get-tuple-element.11), kind=kOutput, calls=%fused_computation.33 | convolution fusion | flops 4311744512 | bytes 12582912 | tf_op jit(solution)/shard_map/dot_general | solution.py:55
  439.6 6.8 %fusion.31 = f32[1,1024,1024]{2,1,0:T(8,128)} fusion(bf16[1024,1024]{1,0:T(8,128)(2,1)S(1)} %get-tuple-element.19, bf16[1024,1024]{1,0:T(8,128)(2,1)S(1)} %get-tuple-element.20, bf16[1024,1024]{1,0:T(8,128)(2,1)S(1)} %copy-done.1, bf16[1024,1024]{1,0:T(8,128)(2,1)S(1)} %get-tuple-element.11), kind=kOutput, calls=%fused_computation.34 | convolution fusion | flops 4311744512 | bytes 12582912 | tf_op jit(solution)/shard_map/dot_general | solution.py:52
  446.3 1.7 maximum_bitcast_fusion.1
  448.0 3.4 maximum_bitcast_fusion
  451.4 6.2 %pad_maximum_fusion = f32[2,2,1024,1024]{3,2,1,0:T(8,128)} fusion(f32[1,2,1024,1024]{3,2,1,0:T(8,128)S(1)} %maximum_bitcast_fusion.1, f32[1,2,1024,1024]{3,2,1,0:T(8,128)S(1)} %maximum_bitcast_fusion), kind=kLoop, calls=%fused_computation | loop fusion | flops 4194304 | bytes 33554432 | tf_op jit(solution)/shard_map/stack | solution.py:57
  (19 shorter events, 0.2 us)
Async XLA Ops:
  6.5 55.3 %all-gather.4.cloned.1.call-start = ((), (), s32[]{:S(2)}) async-start(), calls=%async_computation | async-start | bytes 4456448 | tf_op jit(solution)/shard_map/all_gather | solution.py:62
  7.3 399.0 %all-gather.6.cloned.1.call-start = ((), (), s32[]{:S(2)}) async-start(), calls=%async_computation.1 | async-start | bytes 37748736 | tf_op jit(solution)/shard_map/all_gather | solution.py:8
  64.1 0.7 copy-start.4
  64.1 0.8 copy-start.3
  64.1 0.9 copy-start.5
  64.1 0.9 copy-start.2
  65.0 8.2 %copy-start = (bf16[2,1024,1024]{2,1,0:T(8,128)(2,1)S(1)}, bf16[2,1024,1024]{2,1,0:T(8,128)(2,1)}, u32[]{:S(2)}) copy-start(bf16[2,1024,1024]{2,1,0:T(8,128)(2,1)} %all-gather.4.cloned.1.call-done) | copy-start | bytes 12582916
  423.7 1.6 copy-start.1
Sparse Core Ops, SparseCore 0:
  9.0 52.7 all-gather.3
  64.3 341.9 all-gather.5
